TPU v7x, 256 devices: a whole 4x4x8 slice. The times are simulated.
256 devices in a mesh: pipe: 4 (over y), expert: 16 (over z, core), dp: 4 (over x).
Axes of the slice: x: 4, y: 4, z: 8, core: 2. Of those that a mesh axis runs over, the one named last changes fastest.
Arguments:
- normed: bfloat16 [4, 4, 3072, 4096], P('pipe', None, ('expert', 'dp')), may hold values from -1.5 to 1.5
- saved_out: bfloat16 [4, 4, 3072, 2, 4096], P('pipe', None, ('expert', 'dp')), may hold values from -0.59765625 to 0.59765625
- expert_grads: bfloat16 [4, 4, 4, 16, 16, 9, 4096], P('pipe', None, 'dp', 'expert'), may hold values from -24 to 24
- routes: int32 [4, 4, 3072, 2], P('pipe', None, ('expert', 'dp')), may hold values from 0 to 15, all different within a row; in each aligned block of 48 rows (0 to 47, 48 to 95, ..., all dimensions but the last counted through in order) at most 9 rows name the same one
- router_weight: bfloat16 [4, 4096, 16], P('pipe'), may hold values from -0.375 to 0.375
- upstream: bfloat16 [4, 3072, 4096], P(None, ('expert', 'dp')), may hold values from -6 to 6
Outputs:
- grad_input: bfloat16 [4, 4, 3072, 4096], P('pipe', None, ('expert', 'dp'))
- router_grad: float32 [4, 4096, 16], P('pipe')
Inputs may be any that keep to these rules, and one draw needn't show every extreme that they name: `routes`: the two experts of a row differ. Within the 48 rows of one device for one section and micro-batch no expert is named more than 9 times, a bound that some expert reaches in some of these blocks.
All inputs are finite; a program needn't handle non-finite values.
Results may differ from a plain program's by a relative error of at most 0.007.
Values may be sent and summed in bfloat16 or wider, within the bound.
No kernel may reach another device: no remote copies, remote signals or barrier semaphores. Data moves between devices by JAX's collectives and lax.ppermute only.
A program may use at most 128 MiB of HBM per device.

v0:
```python
import jax
import jax.numpy as jnp
from jax import lax
from jax.sharding import PartitionSpec as P


def shifted(block, axis, distance):
    devices = range(lax.axis_size(axis))
    route = [(i - distance, i) for i in devices if i - distance in devices]
    return lax.ppermute(block, axis, route)


def slot_index(flat, experts, capacity):
    onehot = (flat[..., None] == jnp.arange(experts, dtype=jnp.int32)).astype(jnp.int32)
    before = jnp.cumsum(onehot, axis=-2) - onehot
    position = jnp.sum(before * onehot, axis=-1)
    return flat * capacity + position


def block_grad(incoming, normed_rows, saved_rows, route_rows, returned, index_rows, router_w):
    experts = router_w.shape[1]
    rows_dev = normed_rows.shape[0]
    width = normed_rows.shape[1]
    logits = jnp.dot(normed_rows, router_w, preferred_element_type=jnp.float32)
    expl = jnp.exp(logits)
    probs = expl / jnp.sum(expl, axis=-1, keepdims=True)
    chosen = (route_rows[..., None] == jnp.arange(experts, dtype=jnp.int32)).astype(jnp.float32)
    gates = jnp.einsum("tke,te->tk", chosen, probs)
    dot_grads = jnp.einsum("td,tkd->tk", incoming, saved_rows, preferred_element_type=jnp.float32)
    weighted = dot_grads * gates
    dense_f = (
        jnp.einsum("tke,tk->te", chosen, weighted) - probs * jnp.sum(weighted, axis=-1)[:, None]
    )
    dense = dense_f.astype(jnp.bfloat16)
    router_term = lax.dot_general(
        dense, router_w, (((1,), (1,)), ((), ())), preferred_element_type=jnp.float32
    )
    back_rows = returned[index_rows].reshape(rows_dev, 2, width).astype(jnp.float32)
    total = (
        incoming.astype(jnp.float32)
        + gates[:, 0, None] * back_rows[:, 0]
        + gates[:, 1, None] * back_rows[:, 1]
        + router_term
    )
    weight_part = lax.dot_general(
        normed_rows, dense, (((0,), (0,)), ((), ())), preferred_element_type=jnp.float32
    )
    return (total.astype(jnp.bfloat16), weight_part)


def on_device(normed, saved_out, expert_grads, routes, router_weight, upstream):
    micro = normed.shape[1]
    rows_dev = normed.shape[2]
    width = normed.shape[3]
    sections = lax.axis_size("pipe")
    section_idx = lax.axis_index("pipe")
    router_w = router_weight[0]
    experts = router_w.shape[1]
    capacity = expert_grads.shape[5]
    slot_rows = slot_index(routes[0].reshape(micro, -1), experts, capacity)
    local_grads = expert_grads[0, :, 0]
    returned_list = []
    for block_num in range(micro):
        received = lax.all_to_all(
            local_grads[block_num], "expert", split_axis=1, concat_axis=0, tiled=True
        )
        returned_list.append(received.reshape(experts * capacity, width))
    returned_all = jnp.stack(returned_list)
    grad_buffer = jnp.zeros((micro, rows_dev, width), jnp.bfloat16)
    weight_sum = jnp.zeros((width, experts), jnp.float32)
    passed = jnp.zeros((rows_dev, width), jnp.bfloat16)
    for tick_num in range(micro + sections - 1):
        if tick_num > 0:
            passed = shifted(passed, "pipe", -1)
        block_num = tick_num - (sections - 1 - section_idx)
        is_active = (block_num >= 0) & (block_num < micro)
        block_idx = jnp.clip(block_num, 0, micro - 1)
        returned = lax.dynamic_index_in_dim(returned_all, block_idx, 0, keepdims=False)
        from_top = lax.dynamic_index_in_dim(upstream, block_idx, 0, keepdims=False)
        incoming = jnp.where(section_idx == sections - 1, from_top, passed)
        new_grad, weight_part = block_grad(
            incoming,
            lax.dynamic_index_in_dim(normed[0], block_idx, 0, keepdims=False),
            lax.dynamic_index_in_dim(saved_out[0], block_idx, 0, keepdims=False),
            lax.dynamic_index_in_dim(routes[0], block_idx, 0, keepdims=False),
            returned,
            lax.dynamic_index_in_dim(slot_rows, block_idx, 0, keepdims=False),
            router_w,
        )
        updated = lax.dynamic_update_index_in_dim(grad_buffer, new_grad, block_idx, 0)
        grad_buffer = jnp.where(is_active, updated, grad_buffer)
        weight_sum = weight_sum + jnp.where(is_active, weight_part, 0.0)
        passed = new_grad
    router_grad = lax.psum(weight_sum / micro, ("expert", "dp"))
    return (grad_buffer[None], router_grad[None])


def solution(mesh):
    in_specs = (
        P("pipe", None, ("expert", "dp"), None),
        P("pipe", None, ("expert", "dp"), None, None),
        P("pipe", None, "dp", "expert", None, None, None),
        P("pipe", None, ("expert", "dp"), None),
        P("pipe", None, None),
        P(None, ("expert", "dp"), None),
    )
    out_specs = (P("pipe", None, ("expert", "dp"), None), P("pipe", None, None))
    return jax.shard_map(
        on_device, mesh=mesh, in_specs=in_specs, out_specs=out_specs, check_vma=False
    )
```

profile of v0, /device:TPU:1, one launch (start us, length us, event | category | flops | bytes accessed | tf_op | source)
XLA Modules:
  0.0 636.1 jit_solution(2353032965511129839)
XLA Ops:
  7.2 4.4 fusion.196
  13.7 10.1 %all-to-all-start = ((bf16[1,16,9,4096]{3,2,0,1:T(8,128)(2,1)}), bf16[1,16,9,4096]{3,2,0,1:T(8,128)(2,1)}, u32[]{:S(2)}, u32[]{:S(2)}) async-start(bf16[1,16,9,4096]{3,2,0,1:T(8,128)(2,1)} %bitcast.551), calls=%async_computation | async-start | bytes 4194304 | tf_op jit(solution)/shard_map/all_to_all | solution.py:64
  39.4 33.5 %all-to-all-done = bf16[1,16,9,4096]{3,2,0,1:T(8,128)(2,1)} async-done(((bf16[1,16,9,4096]{3,2,0,1:T(8,128)(2,1)}), bf16[1,16,9,4096]{3,2,0,1:T(8,128)(2,1)}, u32[]{:S(2)}, u32[]{:S(2)}) %all-to-all-start) | async-done | bytes 1179680 | tf_op jit(solution)/shard_map/all_to_all | solution.py:64
  72.9 5.0 all-to-all-start.1
  78.8 3.5 copy.365
  97.5 29.4 %all-to-all-done.1 = bf16[1,16,9,4096]{3,2,0,1:T(8,128)(2,1)} async-done(((bf16[1,16,9,4096]{3,2,0,1:T(8,128)(2,1)}), bf16[1,16,9,4096]{3,2,0,1:T(8,128)(2,1)}, u32[]{:S(2)}, u32[]{:S(2)}) %all-to-all-start.1) | async-done | bytes 1179680 | tf_op jit(solution)/shard_map/all_to_all | solution.py:64
  126.9 5.0 all-to-all-start.2
  143.3 37.7 %all-to-all-done.2 = bf16[1,16,9,4096]{3,2,0,1:T(8,128)(2,1)} async-done(((bf16[1,16,9,4096]{3,2,0,1:T(8,128)(2,1)}), bf16[1,16,9,4096]{3,2,0,1:T(8,128)(2,1)}, u32[]{:S(2)}, u32[]{:S(2)}) %all-to-all-start.2) | async-done | bytes 1179680 | tf_op jit(solution)/shard_map/all_to_all | solution.py:64
  181.0 5.1 all-to-all-start.3
  201.4 33.7 %all-to-all-done.3 = bf16[1,16,9,4096]{3,2,0,1:T(8,128)(2,1)} async-done(((bf16[1,16,9,4096]{3,2,0,1:T(8,128)(2,1)}), bf16[1,16,9,4096]{3,2,0,1:T(8,128)(2,1)}, u32[]{:S(2)}, u32[]{:S(2)}) %all-to-all-start.3) | async-done | bytes 1179680 | tf_op jit(solution)/shard_map/all_to_all | solution.py:64
  240.2 7.0 %dynamic-slice_bitcast_fusion = (bf16[144,4096]{1,0:T(8,128)(2,1)}, bf16[144,4096]{1,0:T(8,128)(2,1)}, bf16[144,4096]{1,0:T(8,128)(2,1)}, bf16[144,4096]{1,0:T(8...) fusion(bf16[4,144,4096]{2,1,0:T(8,128)(2,1)} %constant_dynamic-update-slice_fusion, ...), kind=kLoop, calls=%fused_computation.28 | loop fusion | bytes 16515100 | tf_op jit(solution)/shard_map/jit(dynamic_index_in_dim)/squeeze | solution.py:78
  247.1 4.1 gather_fusion
  254.2 3.6 fusion.203
  263.8 4.2 gather_fusion.1
  271.0 4.7 fusion.202
  275.7 4.2 gather_fusion.2
  282.9 4.7 fusion.201
  287.6 4.2 gather_fusion.3
  294.9 4.7 fusion.200
  299.6 4.3 gather_fusion.4
  319.0 3.8 fusion.81
  327.1 4.2 gather_fusion.5
  348.2 3.8 fusion.78
  356.2 4.3 gather_fusion.6
  375.8 3.6 fusion.75
  385.9 4.9 collective-permute-done.3
  395.4 3.7 fusion.72
  400.8 8.6 %collective-permute-done.4 = bf16[48,4096]{1,0:T(8,128)(2,1)S(1)} collective-permute-done((bf16[48,4096]{1,0:T(8,128)(2,1)S(1)}, bf16[48,4096]{1,0:T(8,128)(2,1)S(1)}, u32[]{:S(2)}, u32[]{:S(2)}) %collective-permute-start.4) | collective-permute-done | bytes 393248 | tf_op jit(solution)/shard_map/ppermute | solution.py:10
  421.9 3.6 fusion.69
  430.0 4.8 collective-permute-done.5
  449.5 3.5 fusion.66
  453.1 174.1 %all-reduce.2.cloned.1.call-done = f32[1,4096,16]{1,2,0:T(8,128)} async-done(((f32[1,4096,16]{1,2,0:T(8,128)}), f32[1,4096,16]{1,2,0:T(8,128)}) %all-reduce.2.cloned.1.call-update) | async-done | bytes 262160 | tf_op jit(solution)/shard_map/psum | solution.py:94
  (286 shorter events, 184.7 us)
Async XLA Ops:
  7.2 20.7 %copy-start = (bf16[1,4,48,2,4096]{4,3,2,1,0:T(2,128)(2,1)S(1)}, bf16[1,4,48,2,4096]{4,3,2,1,0:T(2,128)(2,1)}, u32[]{:S(2)}) copy-start(bf16[1,4,48,2,4096]{4,3,2,1,0:T(2,128)(2,1)} %param.7) | copy-start | bytes 9437188
  13.7 10.1 %copy-start.43 = (s32[1,4,48,2]{2,3,1,0:T(2,128)S(1)}, s32[1,4,48,2]{2,3,1,0:T(2,128)}, u32[]{:S(2)}) copy-start(s32[1,4,48,2]{2,3,1,0:T(2,128)} %param.9) | copy-start | bytes 4612
  13.7 10.9 %copy-start.1 = (bf16[1,4096,16]{1,2,0:T(8,128)(2,1)S(1)}, bf16[1,4096,16]{1,2,0:T(8,128)(2,1)}, u32[]{:S(2)}) copy-start(bf16[1,4096,16]{1,2,0:T(8,128)(2,1)} %param.10) | copy-start | bytes 393220
  13.7 59.2 %all-to-all-start = ((bf16[1,16,9,4096]{3,2,0,1:T(8,128)(2,1)}), bf16[1,16,9,4096]{3,2,0,1:T(8,128)(2,1)}, u32[]{:S(2)}, u32[]{:S(2)}) async-start(bf16[1,16,9,4096]{3,2,0,1:T(8,128)(2,1)} %bitcast.551), calls=%async_computation | async-start | bytes 4194304 | tf_op jit(solution)/shard_map/all_to_all | solution.py:64
  34.2 38.7 %copy-start.41 = (s32[4,96]{1,0:T(4,128)}, s32[4,96]{1,0:T(4,128)S(1)}, u32[]{:S(2)}) copy-start(s32[4,96]{1,0:T(4,128)S(1)} %copy.75) | copy-start | bytes 4612
  34.3 38.6 %copy-start.20 = (s32[48,2]{1,0:T(8,128)}, s32[48,2]{1,0:T(8,128)S(1)}, u32[]{:S(2)}) copy-start(s32[48,2]{1,0:T(8,128)S(1)} %copy.79) | copy-start | bytes 1156
  36.2 41.6 %copy-start.18 = (s32[48,2]{1,0:T(8,128)}, s32[48,2]{1,0:T(8,128)S(1)}, u32[]{:S(2)}) copy-start(s32[48,2]{1,0:T(8,128)S(1)} %copy.82) | copy-start | bytes 1156
  72.9 54.0 %all-to-all-start.1 = ((bf16[1,16,9,4096]{3,2,0,1:T(8,128)(2,1)}), bf16[1,16,9,4096]{3,2,0,1:T(8,128)(2,1)}, u32[]{:S(2)}, u32[]{:S(2)}) async-start(bf16[1,16,9,4096]{3,2,0,1:T(8,128)(2,1)} %bitcast.550), calls=%async_computation.1 | async-start | bytes 4194304 | tf_op jit(solution)/shard_map/all_to_all | solution.py:64
  96.2 35.7 %copy-start.14 = (s32[48,2]{1,0:T(8,128)}, s32[48,2]{1,0:T(8,128)S(1)}, u32[]{:S(2)}) copy-start(s32[48,2]{1,0:T(8,128)S(1)} %copy.94) | copy-start | bytes 1156
  97.4 29.5 %copy-start.48 = (f32[48]{0:T(128)}, f32[48]{0:T(128)S(1)}, u32[]{:S(2)}) copy-start(f32[48]{0:T(128)S(1)} %get-tuple-element.93) | copy-start | bytes 580
  126.9 54.0 %all-to-all-start.2 = ((bf16[1,16,9,4096]{3,2,0,1:T(8,128)(2,1)}), bf16[1,16,9,4096]{3,2,0,1:T(8,128)(2,1)}, u32[]{:S(2)}, u32[]{:S(2)}) async-start(bf16[1,16,9,4096]{3,2,0,1:T(8,128)(2,1)} %bitcast.549), calls=%async_computation.2 | async-start | bytes 4194304 | tf_op jit(solution)/shard_map/all_to_all | solution.py:64
  132.2 54.2 %copy-start.44 = (f32[48,2]{0,1:T(2,128)}, f32[48,2]{0,1:T(2,128)S(1)}, u32[]{:S(2)}) copy-start(f32[48,2]{0,1:T(2,128)S(1)} %copy.167) | copy-start | bytes 1156
  180.9 6.0 copy-start.32
  181.0 6.0 copy-start.42
  181.0 6.0 copy-start.57
  181.0 6.0 copy-start.60
  181.0 54.2 %all-to-all-start.3 = ((bf16[1,16,9,4096]{3,2,0,1:T(8,128)(2,1)}), bf16[1,16,9,4096]{3,2,0,1:T(8,128)(2,1)}, u32[]{:S(2)}, u32[]{:S(2)}) async-start(bf16[1,16,9,4096]{3,2,0,1:T(8,128)(2,1)} %bitcast.548), calls=%async_computation.3 | async-start | bytes 4194304 | tf_op jit(solution)/shard_map/all_to_all | solution.py:64
  186.1 441.1 %all-reduce.2.cloned.1.call-start = ((), (), s32[]{:S(2)}) async-start(), calls=%async_computation.4 | async-start | bytes 524288 | tf_op jit(solution)/shard_map/psum | solution.py:94
  262.1 44.7 %collective-permute-start = (bf16[48,4096]{1,0:T(8,128)(2,1)}, bf16[48,4096]{1,0:T(8,128)(2,1)}, u32[]{:S(2)}, u32[]{:S(2)}) collective-permute-start(bf16[48,4096]{1,0:T(8,128)(2,1)} %get-tuple-element.72), channel_id=1, source_target_pairs={{64,0},{128,64},{192,128},{65,1},{129,65},{193,129},{66,2},{130,66... | collective-permute-start | bytes 1179656 | tf_op jit(solution)/shard_map/ppermute | solution.py:10
  308.0 10.3 %copy-start.30 = (f32[48,16]{0,1:T(8,128)S(1)}, f32[48,16]{0,1:T(8,128)}, u32[]{:S(2)}) copy-start(f32[48,16]{0,1:T(8,128)} %copy-done.29) | copy-start | bytes 9220
  319.0 5.1 copy-start.4
  322.8 13.2 %collective-permute-start.1 = (bf16[48,4096]{1,0:T(8,128)(2,1)}, bf16[48,4096]{1,0:T(8,128)(2,1)}, u32[]{:S(2)}, u32[]{:S(2)}) collective-permute-start(bf16[48,4096]{1,0:T(8,128)(2,1)} %get-tuple-element.76), channel_id=1, source_target_pairs={{64,0},{128,64},{192,128},{65,1},{129,65},{193,129},{66,2},{130,66... | collective-permute-start | bytes 1179656 | tf_op jit(solution)/shard_map/ppermute | solution.py:10
  337.1 10.3 %copy-start.26 = (f32[48,16]{0,1:T(8,128)S(1)}, f32[48,16]{0,1:T(8,128)}, u32[]{:S(2)}) copy-start(f32[48,16]{0,1:T(8,128)} %copy-done.25) | copy-start | bytes 9220
  352.0 11.6 %collective-permute-start.2 = (bf16[48,4096]{1,0:T(8,128)(2,1)}, bf16[48,4096]{1,0:T(8,128)(2,1)}, u32[]{:S(2)}, u32[]{:S(2)}) collective-permute-start(bf16[48,4096]{1,0:T(8,128)(2,1)} %get-tuple-element.80), channel_id=1, source_target_pairs={{64,0},{128,64},{192,128},{65,1},{129,65},{193,129},{66,2},{130,66... | collective-permute-start | bytes 1179656 | tf_op jit(solution)/shard_map/ppermute | solution.py:10
  364.7 10.3 %copy-start.28 = (f32[48,16]{0,1:T(8,128)S(1)}, f32[48,16]{0,1:T(8,128)}, u32[]{:S(2)}) copy-start(f32[48,16]{0,1:T(8,128)} %copy-done.27) | copy-start | bytes 9220
  375.8 5.3 copy-start.6
  379.4 11.4 %collective-permute-start.3 = (bf16[48,4096]{1,0:T(8,128)(2,1)S(1)}, bf16[48,4096]{1,0:T(8,128)(2,1)S(1)}, u32[]{:S(2)}, u32[]{:S(2)}) collective-permute-start(bf16[48,4096]{1,0:T(8,128)(2,1)S(1)} %get-tuple-element.84), channel_id=1, source_target_pairs={{64,0},{128,64},{192,128},{65,1},{129,65},{193,129},{66,2},{130,66... | collective-permute-start | bytes 1179656 | tf_op jit(solution)/shard_map/ppermute | solution.py:10
  395.4 5.2 copy-start.38
  399.1 10.3 %collective-permute-start.4 = (bf16[48,4096]{1,0:T(8,128)(2,1)S(1)}, bf16[48,4096]{1,0:T(8,128)(2,1)S(1)}, u32[]{:S(2)}, u32[]{:S(2)}) collective-permute-start(bf16[48,4096]{1,0:T(8,128)(2,1)S(1)} %get-tuple-element.88), channel_id=1, source_target_pairs={{64,0},{128,64},{192,128},{65,1},{129,65},{193,129},{66,2},{130,66... | collective-permute-start | bytes 1179656 | tf_op jit(solution)/shard_map/ppermute | solution.py:10
  411.2 10.1 %copy-start.22 = (f32[48,16]{0,1:T(8,128)S(1)}, f32[48,16]{0,1:T(8,128)}, u32[]{:S(2)}) copy-start(f32[48,16]{0,1:T(8,128)} %copy-done.21) | copy-start | bytes 9220
  425.6 9.2 %collective-permute-start.5 = (bf16[48,4096]{1,0:T(8,128)(2,1)S(1)}, bf16[48,4096]{1,0:T(8,128)(2,1)S(1)}, u32[]{:S(2)}, u32[]{:S(2)}) collective-permute-start(bf16[48,4096]{1,0:T(8,128)(2,1)S(1)} %get-tuple-element.92), channel_id=1, source_target_pairs={{64,0},{128,64},{192,128},{65,1},{129,65},{193,129},{66,2},{130,66... | collective-permute-start | bytes 1179656 | tf_op jit(solution)/shard_map/ppermute | solution.py:10
  436.6 10.3 %copy-start.49 = (f32[48]{0:T(128)S(1)}, f32[48]{0:T(128)}, u32[]{:S(2)}) copy-start(f32[48]{0:T(128)} %copy-done.48) | copy-start | bytes 580
  (42 other events, 100.4 us)
Sparse Core Ops, SparseCore 0:
  449.7 177.4 all-reduce.1
where the time goes:
time: 646 us; the launch traced here: 636 us
  waiting for transfers between devices  328 us (51%)
  local copies, waits for them, and re-layouts  165 us (26%)
  matrix products  57.4 us (9%)
  other arithmetic  35.6 us (6%)
  starting transfers between devices  33.9 us (5%)
  between operations  15.2 us (2%)
    psum x1, waiting for transfers between devices, on_device(): router_grad = lax.psum(weight_sum / micro, ('expert', 'dp'))  174 us
    all_to_all x4, waiting for transfers between devices, on_device(): lax.all_to_all(local_grads[block_num], 'expert', split_axis=1, concat_axi...  134 us
    unnamed x150, local copies, waits for them, and re-layouts  34.3 us
    gather x7, local copies, waits for them, and re-layouts, block_grad(): returned[index_rows].reshape(rows_dev, 2, width).astype(jnp.float32)  29.6 us
    slice x7, local copies, waits for them, and re-layouts, block_grad(): back_rows[:, 0]  26.5 us
    all_to_all x4, starting transfers between devices, on_device(): lax.all_to_all(local_grads[block_num], 'expert', split_axis=1, concat_axi...  25.2 us
    dot_general x7, matrix products, block_grad(): lax.dot_general(dense, router_w, (((1,), (1,)), ((), ())), preferred_elem...  25 us
    convert_element_type x7, local copies, waits for them, and re-layouts, block_grad(): returned[index_rows].reshape(rows_dev, 2, width).astype(jnp.float32)  20.9 us
  transfers between devices with their start and end apart: 11, of which 10 were waited for; matrix products, arithmetic and copies ran while one was open for 21% of the time, Pallas kernels for 0%

commit v1 on v0

--- a/solution.py
+++ b/solution.py
@@ -91,7 +91,7 @@
         grad_buffer = jnp.where(is_active, updated, grad_buffer)
         weight_sum = weight_sum + jnp.where(is_active, weight_part, 0.0)
         passed = new_grad
-    router_grad = lax.psum(weight_sum / micro, ("expert", "dp"))
+    router_grad = jnp.sum(lax.all_gather(weight_sum / micro, ("expert", "dp")), axis=0)
     return (grad_buffer[None], router_grad[None])
 
 

time: 646 us -> 582 us (0.901)
  waiting for transfers between devices: 328 us -> 245 us
  local copies, waits for them, and re-layouts: 165 us -> 178 us
  other arithmetic: 35.6 us -> 43.7 us
    psum x1 -> x0, waiting for transfers between devices: 174 us -> none  [on_device(): router_grad = lax.psum(weight_sum / micro, ('expert', 'dp'))]
    all_gather x0 -> x1, waiting for transfers between devices: none -> 85.4 us  [on_device(): lax.all_gather(weight_sum / micro, ('expert', 'dp'))]
    unnamed x150 -> x156, local copies, waits for them, and re-layouts: 34.3 us -> 49.2 us
    reduce_sum x0 -> x1, other arithmetic: none -> 8.7 us  [on_device(): jnp.sum(lax.all_gather(weight_sum / micro, ('expert', 'dp')), axis=0)]
  transfers between devices with their start and end apart: 11 -> 11, of which waited for: 10 -> 9; matrix products, arithmetic and copies ran while one was open for 21% -> 23% of each run, Pallas kernels for 0% -> 0%
where the time goes in v1:
time: 582 us; the launch traced here: 572 us
  waiting for transfers between devices  245 us (42%)
  local copies, waits for them, and re-layouts  178 us (31%)
  matrix products  56.8 us (10%)
  other arithmetic  43.7 us (8%)
  starting transfers between devices  34.2 us (6%)
  between operations  15 us (3%)
    all_to_all x4, waiting for transfers between devices, on_device(): lax.all_to_all(local_grads[block_num], 'expert', split_axis=1, concat_axi...  136 us
    all_gather x1, waiting for transfers between devices, on_device(): lax.all_gather(weight_sum / micro, ('expert', 'dp'))  85.4 us
    unnamed x156, local copies, waits for them, and re-layouts  49.2 us
    gather x7, local copies, waits for them, and re-layouts, block_grad(): returned[index_rows].reshape(rows_dev, 2, width).astype(jnp.float32)  29.4 us
    slice x7, local copies, waits for them, and re-layouts, block_grad(): back_rows[:, 0]  25.3 us
    all_to_all x4, starting transfers between devices, on_device(): lax.all_to_all(local_grads[block_num], 'expert', split_axis=1, concat_axi...  25.2 us
    dot_general x7, matrix products, block_grad(): lax.dot_general(dense, router_w, (((1,), (1,)), ((), ())), preferred_elem...  24.5 us
    ppermute x6, waiting for transfers between devices, shifted(): return lax.ppermute(block, axis, route)  23 us
  transfers between devices with their start and end apart: 11, of which 9 were waited for; matrix products, arithmetic and copies ran while one was open for 23% of the time, Pallas kernels for 0%

profile of v1, /device:TPU:1, one launch (start us, length us, event | category | flops | bytes accessed | tf_op | source)
XLA Modules:
  0.0 571.8 jit_solution(3368634060663032119)
XLA Ops:
  7.2 4.4 fusion.195
  13.7 10.1 %all-to-all-start = ((bf16[1,16,9,4096]{3,2,0,1:T(8,128)(2,1)}), bf16[1,16,9,4096]{3,2,0,1:T(8,128)(2,1)}, u32[]{:S(2)}, u32[]{:S(2)}) async-start(bf16[1,16,9,4096]{3,2,0,1:T(8,128)(2,1)} %bitcast.555), calls=%async_computation | async-start | bytes 4194304 | tf_op jit(solution)/shard_map/all_to_all | solution.py:64
  46.1 26.7 %all-to-all-done = bf16[1,16,9,4096]{3,2,0,1:T(8,128)(2,1)} async-done(((bf16[1,16,9,4096]{3,2,0,1:T(8,128)(2,1)}), bf16[1,16,9,4096]{3,2,0,1:T(8,128)(2,1)}, u32[]{:S(2)}, u32[]{:S(2)}) %all-to-all-start) | async-done | bytes 1179680 | tf_op jit(solution)/shard_map/all_to_all | solution.py:64
  72.9 5.0 all-to-all-start.1
  89.3 37.6 %all-to-all-done.1 = bf16[1,16,9,4096]{3,2,0,1:T(8,128)(2,1)} async-done(((bf16[1,16,9,4096]{3,2,0,1:T(8,128)(2,1)}), bf16[1,16,9,4096]{3,2,0,1:T(8,128)(2,1)}, u32[]{:S(2)}, u32[]{:S(2)}) %all-to-all-start.1) | async-done | bytes 1179680 | tf_op jit(solution)/shard_map/all_to_all | solution.py:64
  126.9 5.0 all-to-all-start.2
  142.9 38.1 %all-to-all-done.2 = bf16[1,16,9,4096]{3,2,0,1:T(8,128)(2,1)} async-done(((bf16[1,16,9,4096]{3,2,0,1:T(8,128)(2,1)}), bf16[1,16,9,4096]{3,2,0,1:T(8,128)(2,1)}, u32[]{:S(2)}, u32[]{:S(2)}) %all-to-all-start.2) | async-done | bytes 1179680 | tf_op jit(solution)/shard_map/all_to_all | solution.py:64
  181.0 5.1 all-to-all-start.3
  201.4 33.7 %all-to-all-done.3 = bf16[1,16,9,4096]{3,2,0,1:T(8,128)(2,1)} async-done(((bf16[1,16,9,4096]{3,2,0,1:T(8,128)(2,1)}), bf16[1,16,9,4096]{3,2,0,1:T(8,128)(2,1)}, u32[]{:S(2)}, u32[]{:S(2)}) %all-to-all-start.3) | async-done | bytes 1179680 | tf_op jit(solution)/shard_map/all_to_all | solution.py:64
  240.2 7.0 %dynamic-slice_bitcast_fusion = (bf16[144,4096]{1,0:T(8,128)(2,1)}, bf16[144,4096]{1,0:T(8,128)(2,1)}, bf16[144,4096]{1,0:T(8,128)(2,1)}, bf16[144,4096]{1,0:T(8...) fusion(bf16[4,144,4096]{2,1,0:T(8,128)(2,1)} %constant_dynamic-update-slice_fusion, ...), kind=kLoop, calls=%fused_computation.28 | loop fusion | bytes 16515100 | tf_op jit(solution)/shard_map/jit(dynamic_index_in_dim)/squeeze | solution.py:78
  247.2 4.1 gather_fusion
  254.2 3.5 fusion.202
  263.8 4.2 gather_fusion.1
  271.0 4.7 fusion.201
  275.7 4.2 gather_fusion.2
  282.8 4.7 fusion.200
  287.6 4.2 gather_fusion.3
  307.1 3.8 fusion.80
  315.1 4.2 gather_fusion.4
  336.3 3.8 fusion.77
  344.4 4.2 gather_fusion.5
  363.8 3.7 fusion.74
  373.7 5.5 collective-permute-done.3
  383.8 3.7 fusion.71
  389.1 8.5 %collective-permute-done.4 = bf16[48,4096]{1,0:T(8,128)(2,1)S(1)} collective-permute-done((bf16[48,4096]{1,0:T(8,128)(2,1)S(1)}, bf16[48,4096]{1,0:T(8,128)(2,1)S(1)}, u32[]{:S(2)}, u32[]{:S(2)}) %collective-permute-start.4) | collective-permute-done | bytes 393248 | tf_op jit(solution)/shard_map/ppermute | solution.py:10
  410.3 3.7 fusion.68
  416.0 7.1 %collective-permute-done.5 = bf16[48,4096]{1,0:T(8,128)(2,1)S(1)} collective-permute-done((bf16[48,4096]{1,0:T(8,128)(2,1)S(1)}, bf16[48,4096]{1,0:T(8,128)(2,1)S(1)}, u32[]{:S(2)}, u32[]{:S(2)}) %collective-permute-start.5) | collective-permute-done | bytes 393248 | tf_op jit(solution)/shard_map/ppermute | solution.py:10
  436.6 4.2 gather_fusion.6
  443.7 3.5 fusion.196
  453.0 85.4 %all-gather.3.cloned.1.call-done = f32[262144,16]{0,1:T(8,128)} async-done(((f32[4096,16]{0,1:T(8,128)}), f32[262144,16]{0,1:T(8,128)}) %all-gather.3.cloned.1.call-update) | async-done | bytes 16777232 | tf_op jit(solution)/shard_map/all_gather | solution.py:94
  538.4 17.7 %copy.220 = f32[2,8,64,4096]{3,2,1,0:T(8,128)} copy(f32[2,8,64,4096]{3,1,2,0:T(8,128)} %bitcast.552) | data formatting | bytes 33554432
  556.1 8.7 %bitcast_reduce_fusion = f32[4096,16]{0,1:T(8,128)} fusion(f32[2,8,64,4096]{3,2,1,0:T(8,128)} %copy.220), kind=kLoop, calls=%fused_computation.7 | loop fusion | flops 4128768 | bytes 17039360 | tf_op jit(solution)/shard_map/reduce_sum | solution.py:94
  (293 shorter events, 186.7 us)
Async XLA Ops:
  7.2 20.7 %copy-start = (bf16[1,4,48,2,4096]{4,3,2,1,0:T(2,128)(2,1)S(1)}, bf16[1,4,48,2,4096]{4,3,2,1,0:T(2,128)(2,1)}, u32[]{:S(2)}) copy-start(bf16[1,4,48,2,4096]{4,3,2,1,0:T(2,128)(2,1)} %param.7) | copy-start | bytes 9437188
  13.7 10.1 %copy-start.1 = (bf16[1,4096,16]{1,2,0:T(8,128)(2,1)S(1)}, bf16[1,4096,16]{1,2,0:T(8,128)(2,1)}, u32[]{:S(2)}) copy-start(bf16[1,4096,16]{1,2,0:T(8,128)(2,1)} %param.10) | copy-start | bytes 393220
  13.7 12.0 %copy-start.45 = (s32[1,4,48,2]{2,3,1,0:T(2,128)S(1)}, s32[1,4,48,2]{2,3,1,0:T(2,128)}, u32[]{:S(2)}) copy-start(s32[1,4,48,2]{2,3,1,0:T(2,128)} %param.9) | copy-start | bytes 4612
  13.7 59.2 %all-to-all-start = ((bf16[1,16,9,4096]{3,2,0,1:T(8,128)(2,1)}), bf16[1,16,9,4096]{3,2,0,1:T(8,128)(2,1)}, u32[]{:S(2)}, u32[]{:S(2)}) async-start(bf16[1,16,9,4096]{3,2,0,1:T(8,128)(2,1)} %bitcast.555), calls=%async_computation | async-start | bytes 4194304 | tf_op jit(solution)/shard_map/all_to_all | solution.py:64
  44.0 28.9 %copy-start.22 = (s32[48,2]{1,0:T(8,128)}, s32[48,2]{1,0:T(8,128)S(1)}, u32[]{:S(2)}) copy-start(s32[48,2]{1,0:T(8,128)S(1)} %copy.79) | copy-start | bytes 1156
  46.1 31.7 %copy-start.29 = (f32[48,16]{0,1:T(8,128)}, f32[48,16]{0,1:T(8,128)S(1)}, u32[]{:S(2)}) copy-start(f32[48,16]{0,1:T(8,128)S(1)} %get-tuple-element.78) | copy-start | bytes 9220
  46.1 31.7 %copy-start.55 = (f32[48]{0:T(128)}, f32[48]{0:T(128)S(1)}, u32[]{:S(2)}) copy-start(f32[48]{0:T(128)S(1)} %get-tuple-element.77) | copy-start | bytes 580
  72.9 54.0 %all-to-all-start.1 = ((bf16[1,16,9,4096]{3,2,0,1:T(8,128)(2,1)}), bf16[1,16,9,4096]{3,2,0,1:T(8,128)(2,1)}, u32[]{:S(2)}, u32[]{:S(2)}) async-start(bf16[1,16,9,4096]{3,2,0,1:T(8,128)(2,1)} %bitcast.556), calls=%async_computation.1 | async-start | bytes 4194304 | tf_op jit(solution)/shard_map/all_to_all | solution.py:64
  87.2 39.7 %copy-start.17 = (s32[48,2]{1,0:T(8,128)}, s32[48,2]{1,0:T(8,128)S(1)}, u32[]{:S(2)}) copy-start(s32[48,2]{1,0:T(8,128)S(1)} %copy.91) | copy-start | bytes 1156
  89.3 42.6 %copy-start.50 = (f32[48]{0:T(128)}, f32[48]{0:T(128)S(1)}, u32[]{:S(2)}) copy-start(f32[48]{0:T(128)S(1)} %get-tuple-element.93) | copy-start | bytes 580
  126.9 54.0 %all-to-all-start.2 = ((bf16[1,16,9,4096]{3,2,0,1:T(8,128)(2,1)}), bf16[1,16,9,4096]{3,2,0,1:T(8,128)(2,1)}, u32[]{:S(2)}, u32[]{:S(2)}) async-start(bf16[1,16,9,4096]{3,2,0,1:T(8,128)(2,1)} %bitcast.554), calls=%async_computation.2 | async-start | bytes 4194304 | tf_op jit(solution)/shard_map/all_to_all | solution.py:64
  132.1 48.9 %copy-start.16 = (s32[48,2]{1,0:T(8,128)}, s32[48,2]{1,0:T(8,128)S(1)}, u32[]{:S(2)}) copy-start(s32[48,2]{1,0:T(8,128)S(1)} %copy.94) | copy-start | bytes 1156
  180.9 5.5 copy-start.47
  180.9 6.1 %copy-start.34 = (f32[48,16]{0,1:T(8,128)S(1)}, f32[48,16]{0,1:T(8,128)}, u32[]{:S(2)}) copy-start(f32[48,16]{0,1:T(8,128)} %copy-done.33) | copy-start | bytes 9220
  180.9 6.1 %copy-start.44 = (f32[48,16]{0,1:T(8,128)S(1)}, f32[48,16]{0,1:T(8,128)}, u32[]{:S(2)}) copy-start(f32[48,16]{0,1:T(8,128)} %copy.107) | copy-start | bytes 9220
  180.9 6.1 %copy-start.58 = (f32[48]{0:T(128)S(1)}, f32[48]{0:T(128)}, u32[]{:S(2)}) copy-start(f32[48]{0:T(128)} %copy-done.57) | copy-start | bytes 580
  180.9 6.1 %copy-start.63 = (f32[48]{0:T(128)S(1)}, f32[48]{0:T(128)}, u32[]{:S(2)}) copy-start(f32[48]{0:T(128)} %get-tuple-element.14) | copy-start | bytes 580
  181.0 54.2 %all-to-all-start.3 = ((bf16[1,16,9,4096]{3,2,0,1:T(8,128)(2,1)}), bf16[1,16,9,4096]{3,2,0,1:T(8,128)(2,1)}, u32[]{:S(2)}, u32[]{:S(2)}) async-start(bf16[1,16,9,4096]{3,2,0,1:T(8,128)(2,1)} %bitcast.553), calls=%async_computation.3 | async-start | bytes 4194304 | tf_op jit(solution)/shard_map/all_to_all | solution.py:64
  186.1 352.3 %all-gather.3.cloned.1.call-start = ((), (), s32[]{:S(2)}) async-start(), calls=%async_computation.4 | async-start | bytes 17039360 | tf_op jit(solution)/shard_map/all_gather | solution.py:94
  262.1 32.8 %collective-permute-start = (bf16[48,4096]{1,0:T(8,128)(2,1)}, bf16[48,4096]{1,0:T(8,128)(2,1)}, u32[]{:S(2)}, u32[]{:S(2)}) collective-permute-start(bf16[48,4096]{1,0:T(8,128)(2,1)} %get-tuple-element.72), channel_id=1, source_target_pairs={{64,0},{128,64},{192,128},{65,1},{129,65},{193,129},{66,2},{130,66... | collective-permute-start | bytes 1179656 | tf_op jit(solution)/shard_map/ppermute | solution.py:10
  296.1 10.3 %copy-start.32 = (f32[48,16]{0,1:T(8,128)S(1)}, f32[48,16]{0,1:T(8,128)}, u32[]{:S(2)}) copy-start(f32[48,16]{0,1:T(8,128)} %copy-done.31) | copy-start | bytes 9220
  310.9 13.2 %collective-permute-start.1 = (bf16[48,4096]{1,0:T(8,128)(2,1)}, bf16[48,4096]{1,0:T(8,128)(2,1)}, u32[]{:S(2)}, u32[]{:S(2)}) collective-permute-start(bf16[48,4096]{1,0:T(8,128)(2,1)} %get-tuple-element.76), channel_id=1, source_target_pairs={{64,0},{128,64},{192,128},{65,1},{129,65},{193,129},{66,2},{130,66... | collective-permute-start | bytes 1179656 | tf_op jit(solution)/shard_map/ppermute | solution.py:10
  325.2 10.3 %copy-start.30 = (f32[48,16]{0,1:T(8,128)S(1)}, f32[48,16]{0,1:T(8,128)}, u32[]{:S(2)}) copy-start(f32[48,16]{0,1:T(8,128)} %copy-done.29) | copy-start | bytes 9220
  340.1 11.7 %collective-permute-start.2 = (bf16[48,4096]{1,0:T(8,128)(2,1)}, bf16[48,4096]{1,0:T(8,128)(2,1)}, u32[]{:S(2)}, u32[]{:S(2)}) collective-permute-start(bf16[48,4096]{1,0:T(8,128)(2,1)} %get-tuple-element.80), channel_id=1, source_target_pairs={{64,0},{128,64},{192,128},{65,1},{129,65},{193,129},{66,2},{130,66... | collective-permute-start | bytes 1179656 | tf_op jit(solution)/shard_map/ppermute | solution.py:10
  352.9 10.2 %copy-start.28 = (f32[48,16]{0,1:T(8,128)S(1)}, f32[48,16]{0,1:T(8,128)}, u32[]{:S(2)}) copy-start(f32[48,16]{0,1:T(8,128)} %copy-done.27) | copy-start | bytes 9220
  367.5 11.7 %collective-permute-start.3 = (bf16[48,4096]{1,0:T(8,128)(2,1)S(1)}, bf16[48,4096]{1,0:T(8,128)(2,1)S(1)}, u32[]{:S(2)}, u32[]{:S(2)}) collective-permute-start(bf16[48,4096]{1,0:T(8,128)(2,1)S(1)} %get-tuple-element.84), channel_id=1, source_target_pairs={{64,0},{128,64},{192,128},{65,1},{129,65},{193,129},{66,2},{130,66... | collective-permute-start | bytes 1179656 | tf_op jit(solution)/shard_map/ppermute | solution.py:10
  383.8 5.2 copy-start.40
  387.4 10.2 %collective-permute-start.4 = (bf16[48,4096]{1,0:T(8,128)(2,1)S(1)}, bf16[48,4096]{1,0:T(8,128)(2,1)S(1)}, u32[]{:S(2)}, u32[]{:S(2)}) collective-permute-start(bf16[48,4096]{1,0:T(8,128)(2,1)S(1)} %get-tuple-element.88), channel_id=1, source_target_pairs={{64,0},{128,64},{192,128},{65,1},{129,65},{193,129},{66,2},{130,66... | collective-permute-start | bytes 1179656 | tf_op jit(solution)/shard_map/ppermute | solution.py:10
  399.4 10.1 %copy-start.24 = (f32[48,16]{0,1:T(8,128)S(1)}, f32[48,16]{0,1:T(8,128)}, u32[]{:S(2)}) copy-start(f32[48,16]{0,1:T(8,128)} %copy-done.23) | copy-start | bytes 9220
  410.3 5.4 copy-start.3
  410.3 5.4 copy-start.42
  413.9 9.2 %collective-permute-start.5 = (bf16[48,4096]{1,0:T(8,128)(2,1)S(1)}, bf16[48,4096]{1,0:T(8,128)(2,1)S(1)}, u32[]{:S(2)}, u32[]{:S(2)}) collective-permute-start(bf16[48,4096]{1,0:T(8,128)(2,1)S(1)} %get-tuple-element.92), channel_id=1, source_target_pairs={{64,0},{128,64},{192,128},{65,1},{129,65},{193,129},{66,2},{130,66... | collective-permute-start | bytes 1179656 | tf_op jit(solution)/shard_map/ppermute | solution.py:10
  (45 other events, 115.1 us)
Sparse Core Ops, SparseCore 0:
  436.7 101.6 all-gather.2
